TPU v7x, 256 devices: a whole 4x4x8 slice. The times are simulated.
256 devices in a mesh: cell: 64 (over x, z, core), blk: 4 (over y).
Axes of the slice: x: 4, y: 4, z: 8, core: 2. Of those that a mesh axis runs over, the one named last changes fastest.
Arguments:
- velocity_modes: bfloat16 [8, 3, 2, 256, 256, 128], P('blk', None, None, None, 'cell'), may hold values from -6 to 6
- block_list: int32 [2, 2], replicated, may hold values from 0 to 2, as said below
- counts: int32 [2], replicated, may hold values from 1 to 64, as said below
Outputs:
- transfer: float32 [192, 256, 128], P('blk', 'cell')
- triad_sums: float32 [2, 64, 64], replicated
Inputs may be any that keep to these rules, and one draw needn't show every extreme that they name: `block_list`: each row (K, L) holds two frequency block numbers with K + L <= 2; no row appears twice. counts[n] offsets 0 .. counts[n] - 1 of block L are live; some listed pair has all 64 offsets live in every draw.
All inputs are finite; a program needn't handle non-finite values.
Results may differ from a plain program's by a relative error of at most 0.0003.
Values may be sent and summed in bfloat16 or wider, within the bound.
A program may use at most 128 MiB of HBM per device.

v0:
```python
import math
import jax
import jax.numpy as jnp
from jax import lax
from jax.sharding import PartitionSpec as P

FBLK = 64
CZ = 16


def with_halo(cells, sides, width):
    for axis, dim in sides:
        count = lax.axis_size(axis)
        ends = count - 1
        head = lax.slice_in_dim(cells, 0, width, axis=dim)
        tail = lax.slice_in_dim(cells, cells.shape[dim] - width, cells.shape[dim], axis=dim)
        cells = jnp.concatenate(
            [
                lax.ppermute(tail, axis, [(i, (i + 1) % count) for i in range(ends)]),
                cells,
                lax.ppermute(head, axis, [((i + 1) % count, i) for i in range(ends)]),
            ],
            axis=dim,
        )
    return cells


def ahead(values, stride):
    filler = jnp.zeros(values.shape[:-1] + (stride,), values.dtype)
    return jnp.concatenate([values[..., stride:], filler], axis=-1)


def behind(values, stride):
    filler = jnp.zeros(values.shape[:-1] + (stride,), values.dtype)
    return jnp.concatenate([filler, values[..., :-stride]], axis=-1)


def group_density(donor_modes, slopes, receiver):
    accumulated = 0.0
    for component in range(3):
        real_sum = 0.0
        imag_sum = 0.0
        for direction in range(3):
            grad_real = slopes[direction][:, component, 0][:, :, None]
            grad_imag = slopes[direction][:, component, 1][:, :, None]
            donor_real = donor_modes[:, direction, 0][:, None]
            donor_imag = donor_modes[:, direction, 1][:, None]
            real_sum = real_sum + donor_real * grad_real - donor_imag * grad_imag
            imag_sum = imag_sum + donor_real * grad_imag + donor_imag * grad_real
        accumulated = (
            accumulated
            + receiver[:, component, 0] * real_sum
            + receiver[:, component, 1] * imag_sum
        )
    return -jnp.sum(accumulated, axis=0)


def per_device(velocity_modes, block_list, counts):
    blocks_here, _, _, freq_count, planes, cross_cells = velocity_modes.shape
    block_width = FBLK
    donors_span = (freq_count // block_width - 1) * block_width
    welch_all = blocks_here * lax.axis_size("blk")
    cells_all = planes * lax.axis_size("cell") * cross_cells
    scale_field = 0.25 / math.sqrt(welch_all * block_width)
    scale_triad = 0.25 / math.sqrt(welch_all * cells_all)
    extended = with_halo(velocity_modes, (("cell", 4),), 1)
    group_size = math.gcd(16, block_width)
    turn_count = block_width // group_size
    z_position = lax.broadcasted_iota(jnp.int32, (cross_cells,), 0) % CZ
    keep_upper = (z_position != CZ - 1).astype(jnp.float32)
    keep_lower = (z_position != 0).astype(jnp.float32)
    offsets_group = jnp.arange(group_size, dtype=jnp.int32)
    transfer = jnp.zeros((donors_span, planes, cross_cells), jnp.float32)
    totals_list = []
    for listed in range(block_list.shape[0]):
        start_k = block_list[listed, 0] * block_width
        start_l = block_list[listed, 1] * block_width
        live_count = counts[listed]
        donor_modes = lax.dynamic_slice_in_dim(velocity_modes, start_k, block_width, 3).astype(
            jnp.float32
        )

        def one_turn(running, turn_index):
            first_freq = start_l + turn_index * group_size
            extended_part = lax.dynamic_slice_in_dim(extended, first_freq, group_size, 3).astype(
                jnp.float32
            )
            inner_part = lax.dynamic_slice_in_dim(velocity_modes, first_freq, group_size, 3).astype(
                jnp.float32
            )
            window = lax.dynamic_slice_in_dim(
                velocity_modes, start_k + first_freq, block_width + group_size - 1, 3
            ).astype(jnp.float32)
            slope_first = (extended_part[..., 2:, :] - extended_part[..., :-2, :]) * 0.5
            slope_second = (ahead(inner_part, CZ) - behind(inner_part, CZ)) * 0.5
            slope_third = (
                ahead(inner_part, 1) * keep_upper - behind(inner_part, 1) * keep_lower
            ) * 0.5
            receiver = jnp.stack(
                [window[:, :, :, offset : offset + block_width] for offset in range(group_size)],
                axis=3,
            )
            density = group_density(donor_modes, (slope_first, slope_second, slope_third), receiver)
            live = turn_index * group_size + offsets_group < live_count
            density = jnp.where(live[:, None, None, None], density, 0.0)
            return (running + jnp.sum(density, axis=0), jnp.sum(density, axis=(2, 3)))

        summed, columns = lax.scan(
            one_turn,
            jnp.zeros((block_width, planes, cross_cells), jnp.float32),
            jnp.arange(turn_count, dtype=jnp.int32),
        )
        current = lax.dynamic_slice_in_dim(transfer, start_k, block_width, 0)
        transfer = lax.dynamic_update_slice_in_dim(transfer, current + summed, start_k, 0)
        totals_list.append(columns.reshape(block_width, block_width).T)
    triads_local = jnp.stack(totals_list) * scale_triad
    triad_sums = lax.psum(triads_local, ("cell", "blk"))
    local_field = transfer * scale_field
    whole_field = lax.psum(local_field, "blk")
    share_rows = donors_span // lax.axis_size("blk")
    field_share = lax.dynamic_slice_in_dim(
        whole_field, lax.axis_index("blk") * share_rows, share_rows, 0
    )
    return (field_share, triad_sums)


def solution(mesh):
    return jax.shard_map(
        per_device,
        mesh=mesh,
        in_specs=(P("blk", None, None, None, "cell", None), P(), P()),
        out_specs=(P("blk", "cell", None), P()),
        check_vma=False,
    )
```

profile of v0, /device:TPU:1, one launch (start us, length us, event | category | flops | bytes accessed | tf_op | source)
XLA Modules:
  0.0 577.8 jit_solution(4235348865583273882)
XLA Ops:
  7.2 5.1 fusion.81
  13.3 4.9 collective-permute-start
  19.3 2.3 collective-permute-start.1
  23.6 3.2 copy.268
  28.8 3.6 dynamic-slice_convert_fusion.6
  32.3 2.5 copy.265
  34.9 2.5 copy.267
  37.5 6.8 %pad_maximum_fusion = bf16[2,3,2,256,6,128]{5,4,3,0,2,1:T(8,128)(2,1)} fusion(bf16[2,3,2,256,1,128]{5,4,3,0,2,1:T(2,128)(2,1)S(1)} %copy.267, bf16[2,3,2,256,1,128]{5,4,3,0,2,1:T(2,128)(2,1)S(1)} %copy.265, bf16[2,3,2,256,4,128]{5,4,3,2,1,0:T(4,128)(2,1)S(1)} %copy-done.2), kind=kLoop, calls=%fused_computation.188 | loop fusion | flops 14155776 | bytes 9437184 | tf_op jit(solution)/shard_map/concatenate | solution.py:17
  44.9 220.3 %while.27 = (s32[]{:T(128)}, f32[64,4,128]{2,0,1:T(8,128)S(1)}, f32[4,16,64]{2,1,0:T(8,128)}, s32[4]{0:T(128)S(1)}, s32[]{:T(128)}, /*index=5*/s32[]{:T(128)}, s...) while((s32[]{:T(128)}, f32[64,4,128]{2,0,1:T(8,128)S(1)}, ...), condition=%wide.region_9.10_spmd.clone, body=%wide.region_5.9_spmd.clone.sunk | while | flops 84912424 | bytes 105542472 | solution.py:108
  52.6 1.4 fusion.265
  60.5 1.3 fusion.271
  64.3 1.3 fusion.274
  69.6 26.0 %fusion.279 = f32[16,64,4,128]{3,2,1,0:T(4,128)S(1)} fusion(f32[2,3,2,16,64,4,128]{6,5,4,0,2,1,3:T(4,128)} %fusion.275, f32[2,64,4,128]{3,2,1,0:T(4,128)S(1)} %get-tuple-element.580, f32[2,64,4,128]{3,2,1,0:T(4,128)S(1)} %get-tuple-element.581, f32[2,64,4,128]{3,2,1,0:T(4,128)S(1)} %get-tuple-element.582, ...), kind=kLoop, calls=%fused_computation.100.clone.1 | loop fusion | flops 81264640 | bytes 30015488 | tf_op jit(solution)/shard_map/while/body/eval_jaxpr/reduce_sum | solution.py:55
  96.3 3.0 fusion.281
  107.7 1.4 fusion.265
  119.4 1.3 fusion.274
  124.7 26.0 %fusion.279 = f32[16,64,4,128]{3,2,1,0:T(4,128)S(1)} fusion(f32[2,3,2,16,64,4,128]{6,5,4,0,2,1,3:T(4,128)} %fusion.275, f32[2,64,4,128]{3,2,1,0:T(4,128)S(1)} %get-tuple-element.580, f32[2,64,4,128]{3,2,1,0:T(4,128)S(1)} %get-tuple-element.581, f32[2,64,4,128]{3,2,1,0:T(4,128)S(1)} %get-tuple-element.582, ...), kind=kLoop, calls=%fused_computation.100.clone.1 | loop fusion | flops 81264640 | bytes 30015488 | tf_op jit(solution)/shard_map/while/body/eval_jaxpr/reduce_sum | solution.py:55
  151.3 3.0 fusion.281
  162.8 1.4 fusion.265
  170.6 1.3 fusion.271
  174.5 1.3 fusion.274
  179.7 26.0 %fusion.279 = f32[16,64,4,128]{3,2,1,0:T(4,128)S(1)} fusion(f32[2,3,2,16,64,4,128]{6,5,4,0,2,1,3:T(4,128)} %fusion.275, f32[2,64,4,128]{3,2,1,0:T(4,128)S(1)} %get-tuple-element.580, f32[2,64,4,128]{3,2,1,0:T(4,128)S(1)} %get-tuple-element.581, f32[2,64,4,128]{3,2,1,0:T(4,128)S(1)} %get-tuple-element.582, ...), kind=kLoop, calls=%fused_computation.100.clone.1 | loop fusion | flops 81264640 | bytes 30015488 | tf_op jit(solution)/shard_map/while/body/eval_jaxpr/reduce_sum | solution.py:55
  206.4 3.0 fusion.281
  217.8 1.4 fusion.265
  229.6 1.3 fusion.274
  234.8 26.0 %fusion.279 = f32[16,64,4,128]{3,2,1,0:T(4,128)S(1)} fusion(f32[2,3,2,16,64,4,128]{6,5,4,0,2,1,3:T(4,128)} %fusion.275, f32[2,64,4,128]{3,2,1,0:T(4,128)S(1)} %get-tuple-element.580, f32[2,64,4,128]{3,2,1,0:T(4,128)S(1)} %get-tuple-element.581, f32[2,64,4,128]{3,2,1,0:T(4,128)S(1)} %get-tuple-element.582, ...), kind=kLoop, calls=%fused_computation.100.clone.1 | loop fusion | flops 81264640 | bytes 30015488 | tf_op jit(solution)/shard_map/while/body/eval_jaxpr/reduce_sum | solution.py:55
  261.5 3.0 fusion.281
  265.8 221.3 %while.26 = (s32[]{:T(128)}, f32[64,4,128]{2,0,1:T(8,128)S(1)}, f32[4,16,64]{2,1,0:T(8,128)}, s32[4]{0:T(128)S(1)}, s32[]{:T(128)}, /*index=5*/s32[]{:T(128)}, s...) while((s32[]{:T(128)}, f32[64,4,128]{2,0,1:T(8,128)S(1)}, ...), condition=%wide.region_4.5_spmd.clone, body=%wide.region_0.4_spmd.clone.sunk | while | flops 84912424 | bytes 105542472 | solution.py:108
  273.7 1.4 fusion.225
  281.6 1.3 fusion.231
  285.5 1.3 fusion.234
  290.7 26.0 %fusion.239 = f32[16,64,4,128]{3,2,1,0:T(4,128)S(1)} fusion(f32[2,3,2,16,64,4,128]{6,5,4,0,2,1,3:T(4,128)} %fusion.235, f32[2,64,4,128]{3,2,1,0:T(4,128)S(1)} %get-tuple-element.538, f32[2,64,4,128]{3,2,1,0:T(4,128)S(1)} %get-tuple-element.539, f32[2,64,4,128]{3,2,1,0:T(4,128)S(1)} %get-tuple-element.540, ...), kind=kLoop, calls=%fused_computation.9.clone.1 | loop fusion | flops 81264640 | bytes 30015488 | tf_op jit(solution)/shard_map/while/body/eval_jaxpr/reduce_sum | solution.py:55
  317.4 3.0 fusion.241
  329.1 1.4 fusion.225
  336.9 1.3 fusion.231
  340.8 1.3 fusion.234
  346.0 26.0 %fusion.239 = f32[16,64,4,128]{3,2,1,0:T(4,128)S(1)} fusion(f32[2,3,2,16,64,4,128]{6,5,4,0,2,1,3:T(4,128)} %fusion.235, f32[2,64,4,128]{3,2,1,0:T(4,128)S(1)} %get-tuple-element.538, f32[2,64,4,128]{3,2,1,0:T(4,128)S(1)} %get-tuple-element.539, f32[2,64,4,128]{3,2,1,0:T(4,128)S(1)} %get-tuple-element.540, ...), kind=kLoop, calls=%fused_computation.9.clone.1 | loop fusion | flops 81264640 | bytes 30015488 | tf_op jit(solution)/shard_map/while/body/eval_jaxpr/reduce_sum | solution.py:55
  372.8 3.0 fusion.241
  384.4 1.4 fusion.225
  396.1 1.3 fusion.234
  401.4 26.0 %fusion.239 = f32[16,64,4,128]{3,2,1,0:T(4,128)S(1)} fusion(f32[2,3,2,16,64,4,128]{6,5,4,0,2,1,3:T(4,128)} %fusion.235, f32[2,64,4,128]{3,2,1,0:T(4,128)S(1)} %get-tuple-element.538, f32[2,64,4,128]{3,2,1,0:T(4,128)S(1)} %get-tuple-element.539, f32[2,64,4,128]{3,2,1,0:T(4,128)S(1)} %get-tuple-element.540, ...), kind=kLoop, calls=%fused_computation.9.clone.1 | loop fusion | flops 81264640 | bytes 30015488 | tf_op jit(solution)/shard_map/while/body/eval_jaxpr/reduce_sum | solution.py:55
  428.1 3.0 fusion.241
  439.7 1.4 fusion.225
  451.4 1.3 fusion.234
  456.7 26.0 %fusion.239 = f32[16,64,4,128]{3,2,1,0:T(4,128)S(1)} fusion(f32[2,3,2,16,64,4,128]{6,5,4,0,2,1,3:T(4,128)} %fusion.235, f32[2,64,4,128]{3,2,1,0:T(4,128)S(1)} %get-tuple-element.538, f32[2,64,4,128]{3,2,1,0:T(4,128)S(1)} %get-tuple-element.539, f32[2,64,4,128]{3,2,1,0:T(4,128)S(1)} %get-tuple-element.540, ...), kind=kLoop, calls=%fused_computation.9.clone.1 | loop fusion | flops 81264640 | bytes 30015488 | tf_op jit(solution)/shard_map/while/body/eval_jaxpr/reduce_sum | solution.py:55
  483.4 3.0 fusion.241
  489.1 79.7 %psum.15 = f32[2,64,64]{1,2,0:T(8,128)S(1)} all-reduce(f32[2,64,64]{1,2,0:T(8,128)S(1)} %maximum_multiply_fusion), channel_id=1, replica_groups=mesh['cell'=64,'blk'=4] {'cell','blk'}, use_global_device_ids=true, to_apply=%region_11.12 | all-reduce | flops 8192 | bytes 65536 | tf_op jit(solution)/shard_map/psum | solution.py:117
  569.5 1.5 constant_dynamic-slice_fusion
  (287 shorter events, 183.2 us)
Async XLA Ops:
  7.2 14.5 %copy-start.3 = (s32[2,2]{1,0:T(2,128)S(1)}, s32[2,2]{1,0:T(2,128)}, u32[]{:S(2)}) copy-start(s32[2,2]{1,0:T(2,128)} %param.8) | copy-start | bytes 52
  7.2 562.3 %all-reduce.10.cloned.1.call-start = ((), (), s32[]{:S(2)}) async-start(), calls=%async_computation | async-start | bytes 786432 | tf_op jit(solution)/shard_map/psum | solution.py:119
  13.3 19.0 %collective-permute-start = (bf16[2,3,2,256,1,128]{5,3,4,2,1,0:T(8,128)(2,1)}, bf16[2,3,2,256,1,128]{5,3,4,2,1,0:T(8,128)(2,1)}, u32[]{:S(2)}, u32[]{:S(2)}) collective-permute-start(bf16[2,3,2,256,1,128]{5,3,4,2,1,0:T(8,128)(2,1)} %copy.288), channel_id=1, source_target_pairs={{0,4},{4,8},{8,12},{12,16},{16,20},{20,24},{24,28},{28,32},{32,36}... | collective-permute-start | bytes 2359304 | tf_op jit(solution)/shard_map/ppermute | solution.py:19
  18.2 9.9 %copy-start.4 = (s32[2]{0:T(128)S(1)}, s32[2]{0:T(128)}, u32[]{:S(2)}) copy-start(s32[2]{0:T(128)} %param.9) | copy-start | bytes 28
  19.3 15.6 %collective-permute-start.1 = (bf16[2,3,2,256,1,128]{5,3,4,2,1,0:T(8,128)(2,1)}, bf16[2,3,2,256,1,128]{5,3,4,2,1,0:T(8,128)(2,1)}, u32[]{:S(2)}, u32[]{:S(2)}) collective-permute-start(bf16[2,3,2,256,1,128]{5,3,4,2,1,0:T(8,128)(2,1)} %copy.289), channel_id=1, source_target_pairs={{4,0},{8,4},{12,8},{16,12},{20,16},{24,20},{28,24},{32,28},{36,32}... | collective-permute-start | bytes 2359304 | tf_op jit(solution)/shard_map/ppermute | solution.py:21
  28.8 8.7 %copy-start.2 = (bf16[2,3,2,256,4,128]{5,4,3,2,1,0:T(4,128)(2,1)S(1)}, bf16[2,3,2,256,4,128]{5,4,3,2,1,0:T(4,128)(2,1)}, u32[]{:S(2)}) copy-start(bf16[2,3,2,256,4,128]{5,4,3,2,1,0:T(4,128)(2,1)} %param.7) | copy-start | bytes 9437188
  67.3 2.2 copy-start.1
  122.4 2.2 copy-start.1
  177.4 2.2 copy-start.1
  232.5 2.2 copy-start.1
  288.4 2.2 copy-start
  343.7 2.2 copy-start
  399.1 2.2 copy-start
  454.4 2.2 copy-start
Sparse Core Ops, SparseCore 0:
  488.4 48.5 all-reduce.9
where the time goes:
time: 579 us; the launch traced here: 578 us
  other arithmetic  266 us (46%)
  local copies, waits for them, and re-layouts  202 us (35%)
  blocking collectives  79.7 us (14%)
  between operations  16.8 us (3%)
  starting transfers between devices  7.28 us (1%)
  loops' own time  6.1 us (1%)
    reduce_sum x8, other arithmetic, group_density(): return -jnp.sum(accumulated, axis=0)  208 us
    while x136, local copies, waits for them, and re-layouts  156 us
    psum x1, blocking collectives, per_device(): triad_sums = lax.psum(triads_local, ('cell', 'blk'))  79.7 us
    reduce_sum x8, other arithmetic, one_turn(): return (running + jnp.sum(density, axis=0), jnp.sum(density, axis=(2, 3)))  24.4 us
  transfers between devices with their start and end apart: 3, of which 0 were waited for; matrix products, arithmetic and copies ran while one was open for 2% of the time, Pallas kernels for 0%

commit v1 on v0

--- a/solution.py
+++ b/solution.py
@@ -114,7 +114,7 @@
         transfer = lax.dynamic_update_slice_in_dim(transfer, current + summed, start_k, 0)
         totals_list.append(columns.reshape(block_width, block_width).T)
     triads_local = jnp.stack(totals_list) * scale_triad
-    triad_sums = lax.psum(triads_local, ("cell", "blk"))
+    triad_sums = lax.psum(lax.psum(triads_local, "cell"), "blk")
     local_field = transfer * scale_field
     whole_field = lax.psum(local_field, "blk")
     share_rows = donors_span // lax.axis_size("blk")

time: 579 us -> 766 us (1.32)
  blocking collectives: 79.7 us -> 262 us
    psum x1 -> x2, blocking collectives: 79.7 us -> 262 us  [per_device(): triad_sums = lax.psum(lax.psum(triads_local, 'cell'), 'blk')]
where the time goes in v1:
time: 766 us; the launch traced here: 759 us
  other arithmetic  265 us (35%)
  blocking collectives  262 us (34%)
  local copies, waits for them, and re-layouts  202 us (26%)
  between operations  16.7 us (2%)
    psum x2, blocking collectives, per_device(): triad_sums = lax.psum(lax.psum(triads_local, 'cell'), 'blk')  262 us
    reduce_sum x8, other arithmetic, group_density(): return -jnp.sum(accumulated, axis=0)  208 us
    while x136, local copies, waits for them, and re-layouts  156 us
    reduce_sum x8, other arithmetic, one_turn(): return (running + jnp.sum(density, axis=0), jnp.sum(density, axis=(2, 3)))  24.4 us
  transfers between devices with their start and end apart: 3, of which 0 were waited for; matrix products, arithmetic and copies ran while one was open for 2% of the time, Pallas kernels for 0%

profile of v1, /device:TPU:1, one launch (start us, length us, event | category | flops | bytes accessed | tf_op | source)
XLA Modules:
  0.0 759.1 jit_solution(600797913929713117)
XLA Ops:
  7.2 5.1 fusion.81
  13.3 4.9 collective-permute-start
  19.3 2.3 collective-permute-start.1
  23.6 3.2 copy.268
  28.6 3.6 dynamic-slice_convert_fusion.6
  32.2 2.5 copy.265
  34.8 2.5 copy.267
  37.3 6.8 pad_maximum_fusion
  44.8 220.9 %while.27 = (s32[]{:T(128)}, f32[64,4,128]{2,0,1:T(8,128)S(1)}, f32[4,16,64]{2,1,0:T(8,128)}, s32[4]{0:T(128)S(1)}, s32[]{:T(128)}, /*index=5*/s32[]{:T(128)}, s...) while((s32[]{:T(128)}, f32[64,4,128]{2,0,1:T(8,128)S(1)}, ...), condition=%wide.region_9.10_spmd.clone, body=%wide.region_5.9_spmd.clone.sunk | while | flops 84912424 | bytes 105542472 | solution.py:108
  52.6 1.4 fusion.265
  64.4 1.3 fusion.274
  69.6 26.0 %fusion.279 = f32[16,64,4,128]{3,2,1,0:T(4,128)S(1)} fusion(f32[2,3,2,16,64,4,128]{6,5,4,0,2,1,3:T(4,128)} %fusion.275, f32[2,64,4,128]{3,2,1,0:T(4,128)S(1)} %get-tuple-element.580, f32[2,64,4,128]{3,2,1,0:T(4,128)S(1)} %get-tuple-element.581, f32[2,64,4,128]{3,2,1,0:T(4,128)S(1)} %get-tuple-element.582, ...), kind=kLoop, calls=%fused_computation.100.clone.1 | loop fusion | flops 81264640 | bytes 30015488 | tf_op jit(solution)/shard_map/while/body/eval_jaxpr/reduce_sum | solution.py:55
  96.3 3.0 fusion.281
  107.9 1.4 fusion.265
  111.8 1.3 fusion.268
  119.6 1.3 fusion.274
  124.8 26.0 %fusion.279 = f32[16,64,4,128]{3,2,1,0:T(4,128)S(1)} fusion(f32[2,3,2,16,64,4,128]{6,5,4,0,2,1,3:T(4,128)} %fusion.275, f32[2,64,4,128]{3,2,1,0:T(4,128)S(1)} %get-tuple-element.580, f32[2,64,4,128]{3,2,1,0:T(4,128)S(1)} %get-tuple-element.581, f32[2,64,4,128]{3,2,1,0:T(4,128)S(1)} %get-tuple-element.582, ...), kind=kLoop, calls=%fused_computation.100.clone.1 | loop fusion | flops 81264640 | bytes 30015488 | tf_op jit(solution)/shard_map/while/body/eval_jaxpr/reduce_sum | solution.py:55
  151.5 3.0 fusion.281
  163.1 1.4 fusion.265
  167.0 1.3 fusion.268
  174.8 1.3 fusion.274
  180.1 26.0 %fusion.279 = f32[16,64,4,128]{3,2,1,0:T(4,128)S(1)} fusion(f32[2,3,2,16,64,4,128]{6,5,4,0,2,1,3:T(4,128)} %fusion.275, f32[2,64,4,128]{3,2,1,0:T(4,128)S(1)} %get-tuple-element.580, f32[2,64,4,128]{3,2,1,0:T(4,128)S(1)} %get-tuple-element.581, f32[2,64,4,128]{3,2,1,0:T(4,128)S(1)} %get-tuple-element.582, ...), kind=kLoop, calls=%fused_computation.100.clone.1 | loop fusion | flops 81264640 | bytes 30015488 | tf_op jit(solution)/shard_map/while/body/eval_jaxpr/reduce_sum | solution.py:55
  206.7 3.0 fusion.281
  218.3 1.4 fusion.265
  230.0 1.3 fusion.274
  235.3 26.0 %fusion.279 = f32[16,64,4,128]{3,2,1,0:T(4,128)S(1)} fusion(f32[2,3,2,16,64,4,128]{6,5,4,0,2,1,3:T(4,128)} %fusion.275, f32[2,64,4,128]{3,2,1,0:T(4,128)S(1)} %get-tuple-element.580, f32[2,64,4,128]{3,2,1,0:T(4,128)S(1)} %get-tuple-element.581, f32[2,64,4,128]{3,2,1,0:T(4,128)S(1)} %get-tuple-element.582, ...), kind=kLoop, calls=%fused_computation.100.clone.1 | loop fusion | flops 81264640 | bytes 30015488 | tf_op jit(solution)/shard_map/while/body/eval_jaxpr/reduce_sum | solution.py:55
  262.0 3.0 fusion.281
  266.3 220.2 %while.26 = (s32[]{:T(128)}, f32[64,4,128]{2,0,1:T(8,128)S(1)}, f32[4,16,64]{2,1,0:T(8,128)}, s32[4]{0:T(128)S(1)}, s32[]{:T(128)}, /*index=5*/s32[]{:T(128)}, s...) while((s32[]{:T(128)}, f32[64,4,128]{2,0,1:T(8,128)S(1)}, ...), condition=%wide.region_4.5_spmd.clone, body=%wide.region_0.4_spmd.clone.sunk | while | flops 84912424 | bytes 105542472 | solution.py:108
  274.1 1.4 fusion.225
  278.0 1.3 fusion.228
  285.8 1.3 fusion.234
  291.0 26.0 %fusion.239 = f32[16,64,4,128]{3,2,1,0:T(4,128)S(1)} fusion(f32[2,3,2,16,64,4,128]{6,5,4,0,2,1,3:T(4,128)} %fusion.235, f32[2,64,4,128]{3,2,1,0:T(4,128)S(1)} %get-tuple-element.538, f32[2,64,4,128]{3,2,1,0:T(4,128)S(1)} %get-tuple-element.539, f32[2,64,4,128]{3,2,1,0:T(4,128)S(1)} %get-tuple-element.540, ...), kind=kLoop, calls=%fused_computation.9.clone.1 | loop fusion | flops 81264640 | bytes 30015488 | tf_op jit(solution)/shard_map/while/body/eval_jaxpr/reduce_sum | solution.py:55
  317.6 3.0 fusion.241
  329.1 1.4 fusion.225
  340.8 1.3 fusion.234
  346.1 26.0 %fusion.239 = f32[16,64,4,128]{3,2,1,0:T(4,128)S(1)} fusion(f32[2,3,2,16,64,4,128]{6,5,4,0,2,1,3:T(4,128)} %fusion.235, f32[2,64,4,128]{3,2,1,0:T(4,128)S(1)} %get-tuple-element.538, f32[2,64,4,128]{3,2,1,0:T(4,128)S(1)} %get-tuple-element.539, f32[2,64,4,128]{3,2,1,0:T(4,128)S(1)} %get-tuple-element.540, ...), kind=kLoop, calls=%fused_computation.9.clone.1 | loop fusion | flops 81264640 | bytes 30015488 | tf_op jit(solution)/shard_map/while/body/eval_jaxpr/reduce_sum | solution.py:55
  372.7 3.0 fusion.241
  384.1 1.4 fusion.225
  395.9 1.3 fusion.234
  401.1 26.0 %fusion.239 = f32[16,64,4,128]{3,2,1,0:T(4,128)S(1)} fusion(f32[2,3,2,16,64,4,128]{6,5,4,0,2,1,3:T(4,128)} %fusion.235, f32[2,64,4,128]{3,2,1,0:T(4,128)S(1)} %get-tuple-element.538, f32[2,64,4,128]{3,2,1,0:T(4,128)S(1)} %get-tuple-element.539, f32[2,64,4,128]{3,2,1,0:T(4,128)S(1)} %get-tuple-element.540, ...), kind=kLoop, calls=%fused_computation.9.clone.1 | loop fusion | flops 81264640 | bytes 30015488 | tf_op jit(solution)/shard_map/while/body/eval_jaxpr/reduce_sum | solution.py:55
  427.7 3.0 fusion.241
  439.2 1.4 fusion.225
  450.9 1.3 fusion.234
  456.2 26.0 %fusion.239 = f32[16,64,4,128]{3,2,1,0:T(4,128)S(1)} fusion(f32[2,3,2,16,64,4,128]{6,5,4,0,2,1,3:T(4,128)} %fusion.235, f32[2,64,4,128]{3,2,1,0:T(4,128)S(1)} %get-tuple-element.538, f32[2,64,4,128]{3,2,1,0:T(4,128)S(1)} %get-tuple-element.539, f32[2,64,4,128]{3,2,1,0:T(4,128)S(1)} %get-tuple-element.540, ...), kind=kLoop, calls=%fused_computation.9.clone.1 | loop fusion | flops 81264640 | bytes 30015488 | tf_op jit(solution)/shard_map/while/body/eval_jaxpr/reduce_sum | solution.py:55
  482.8 3.0 fusion.241
  488.5 247.5 %psum.22 = f32[2,64,64]{1,2,0:T(8,128)S(1)} all-reduce(f32[2,64,64]{1,2,0:T(8,128)S(1)} %maximum_multiply_fusion), channel_id=1, replica_groups=mesh['cell'=64,'blk'=4] {'cell'}, use_global_device_ids=true, to_apply=%region_11.12 | all-reduce | flops 8192 | bytes 65536 | tf_op jit(solution)/shard_map/psum | solution.py:117
  736.0 14.0 %psum.23 = f32[2,64,64]{1,2,0:T(8,128)S(1)} all-reduce(f32[2,64,64]{1,2,0:T(8,128)S(1)} %psum.22), channel_id=1, replica_groups=mesh['cell'=64,'blk'=4] {'blk'}, use_global_device_ids=true, to_apply=%region_12.13 | all-reduce | flops 8192 | bytes 65536 | tf_op jit(solution)/shard_map/psum | solution.py:117
  750.7 1.5 constant_dynamic-slice_fusion
  (288 shorter events, 184.2 us)
Async XLA Ops:
  7.2 14.5 %copy-start.3 = (s32[2,2]{1,0:T(2,128)S(1)}, s32[2,2]{1,0:T(2,128)}, u32[]{:S(2)}) copy-start(s32[2,2]{1,0:T(2,128)} %param.8) | copy-start | bytes 52
  7.2 743.6 %all-reduce.10.cloned.1.call-start = ((), (), s32[]{:S(2)}) async-start(), calls=%async_computation | async-start | bytes 786432 | tf_op jit(solution)/shard_map/psum | solution.py:119
  13.3 18.9 %collective-permute-start = (bf16[2,3,2,256,1,128]{5,3,4,2,1,0:T(8,128)(2,1)}, bf16[2,3,2,256,1,128]{5,3,4,2,1,0:T(8,128)(2,1)}, u32[]{:S(2)}, u32[]{:S(2)}) collective-permute-start(bf16[2,3,2,256,1,128]{5,3,4,2,1,0:T(8,128)(2,1)} %copy.288), channel_id=1, source_target_pairs={{0,4},{4,8},{8,12},{12,16},{16,20},{20,24},{24,28},{28,32},{32,36}... | collective-permute-start | bytes 2359304 | tf_op jit(solution)/shard_map/ppermute | solution.py:19
  18.3 9.8 %copy-start.4 = (s32[2]{0:T(128)S(1)}, s32[2]{0:T(128)}, u32[]{:S(2)}) copy-start(s32[2]{0:T(128)} %param.9) | copy-start | bytes 28
  19.3 15.4 %collective-permute-start.1 = (bf16[2,3,2,256,1,128]{5,3,4,2,1,0:T(8,128)(2,1)}, bf16[2,3,2,256,1,128]{5,3,4,2,1,0:T(8,128)(2,1)}, u32[]{:S(2)}, u32[]{:S(2)}) collective-permute-start(bf16[2,3,2,256,1,128]{5,3,4,2,1,0:T(8,128)(2,1)} %copy.289), channel_id=1, source_target_pairs={{4,0},{8,4},{12,8},{16,12},{20,16},{24,20},{28,24},{32,28},{36,32}... | collective-permute-start | bytes 2359304 | tf_op jit(solution)/shard_map/ppermute | solution.py:21
  28.6 8.7 %copy-start.2 = (bf16[2,3,2,256,4,128]{5,4,3,2,1,0:T(4,128)(2,1)S(1)}, bf16[2,3,2,256,4,128]{5,4,3,2,1,0:T(4,128)(2,1)}, u32[]{:S(2)}) copy-start(bf16[2,3,2,256,4,128]{5,4,3,2,1,0:T(4,128)(2,1)} %param.7) | copy-start | bytes 9437188
  67.3 2.2 copy-start.1
  122.6 2.2 copy-start.1
  177.8 2.2 copy-start.1
  233.0 2.2 copy-start.1
  288.7 2.2 copy-start
  343.8 2.2 copy-start
  398.8 2.2 copy-start
  453.9 2.2 copy-start
Sparse Core Ops, SparseCore 0:
  487.8 48.7 all-reduce.9
